TPU v7x, 32 devices: a whole 2x2x4 slice. The times are simulated.
32 devices in a mesh: dp: 4 (over y, x), ctx: 2 (over core), expert: 4 (over z).
Axes of the slice: x: 2, y: 2, z: 4, core: 2. Of those that a mesh axis runs over, the one named last changes fastest.
Arguments:
- tokens: bfloat16 [96, 200, 512], P(('dp', 'expert'), 'ctx'), may hold values from -6 to 6
- gain_one: float32 [512], replicated, may hold values from 0.1 to 1.9
- w_qkv: bfloat16 [512, 1536], replicated, may hold values from -0.25 to 0.25
- w_out: bfloat16 [512, 512], replicated, may hold values from -1 to 1
- gain_two: float32 [512], replicated, may hold values from 0.1 to 1.9
- w_router: bfloat16 [512, 4], replicated, may hold values from -0.1875 to 0.1875
- w_in: bfloat16 [4, 512, 2048], P('expert'), may hold values from -0.25 to 0.25
- w_back: bfloat16 [4, 2048, 512], P('expert'), may hold values from -0.25 to 0.25
- route_ids: int32 [16, 2, 6, 100, 2], P(('dp', 'expert'), 'ctx'), may hold values from 0 to 3, all different within a row; in each aligned block of 600 rows (0 to 599, 600 to 1199, ..., all dimensions but the last counted through in order) at most 600 rows name the same one
- key_mask: int32 [96, 200], P(('dp', 'expert')), may hold values from 0 to 1, as said below
- cotangent: bfloat16 [96, 200, 512], P(('dp', 'expert'), 'ctx'), may hold values from -6 to 6
Outputs:
- mixed: bfloat16 [96, 200, 512], P(('dp', 'expert'), 'ctx')
- grad_tokens: bfloat16 [96, 200, 512], P(('dp', 'expert'), 'ctx')
- grad_gain_one: float32 [512], replicated
- grad_qkv: float32 [512, 1536], replicated
- grad_out: float32 [512, 512], replicated
- grad_gain_two: float32 [512], replicated
- grad_router: float32 [512, 4], replicated
- grad_in: float32 [4, 512, 2048], P('expert')
- grad_back: float32 [4, 2048, 512], P('expert')
Inputs may be any that keep to these rules, and one draw needn't show every extreme that they name: Among the 600 tokens of one device (one aligned block of route_ids), at most 600 routes name the same expert, ; a token's two experts differ. `key_mask`: each image's mask is 1 on a first run of positions of length 150 to 200, then 0.
All inputs are finite; a program needn't handle non-finite values.
Results may differ from a plain program's by a relative error of at most 0.017.
Values may be sent and summed in bfloat16 or wider, within the bound.
No kernel may reach another device: no remote copies, remote signals or barrier semaphores. Data moves between devices by JAX's collectives and lax.ppermute only.
A program may use at most 192 MiB of HBM per device.

v0:
```python
import jax
import jax.numpy as jnp
from jax import lax
from jax.sharding import PartitionSpec as P

HEADS = 8
HEAD_DIM = 64
TOP = 2


def norm_rows(value, gain):
    center = value - jnp.mean(value, -1, keepdims=True)
    spread = jnp.mean(center * center, -1, keepdims=True)
    return center * lax.rsqrt(spread + 1e-06) * gain


def smooth_gelu(value):
    return 0.5 * value * (1.0 + jnp.tanh(0.7978845608 * (value + 0.044715 * value * value * value)))


def forward(tokens, gain_one, w_qkv, w_out, gain_two, w_router, w_in, w_back, flat_ids, live):
    nimg, half, width = tokens.shape
    count = nimg * half
    experts_all = w_router.shape[1]
    capacity = max(2, 2 * TOP * count // experts_all)
    x_rows = tokens.astype(jnp.float32).reshape(count, width)
    normed = norm_rows(x_rows, gain_one).astype(jnp.bfloat16)
    qkv = jnp.dot(normed, w_qkv, preferred_element_type=jnp.float32).astype(jnp.bfloat16)
    qkv = qkv.reshape(nimg, half, 3 * width)
    query = qkv[..., :width]
    keys_local = qkv[..., width : 2 * width]
    vals_local = qkv[..., 2 * width :]
    keys, vals = (
        lax.all_gather(keys_local, "ctx", axis=1, tiled=True),
        lax.all_gather(vals_local, "ctx", axis=1, tiled=True),
    )
    seq = keys.shape[1]
    query4 = query.reshape(nimg, half, HEADS, HEAD_DIM)
    keys4 = keys.reshape(nimg, seq, HEADS, HEAD_DIM)
    vals4 = vals.reshape(nimg, seq, HEADS, HEAD_DIM)
    scale = HEAD_DIM ** (-0.5)
    scores = (
        jnp.einsum("iqhc,ikhc->ihqk", query4, keys4, preferred_element_type=jnp.float32) * scale
    )
    open_keys = live[:, None, None, :]
    masked = jnp.where(open_keys, scores, -1000000000.0)
    topmost = jnp.max(masked, -1, keepdims=True)
    expo = jnp.where(open_keys, jnp.exp(masked - topmost), 0.0)
    probs = expo / jnp.sum(expo, -1, keepdims=True)
    probs_low = probs.astype(jnp.bfloat16)
    mix = jnp.einsum("ihqk,ikhc->iqhc", probs_low, vals4, preferred_element_type=jnp.float32)
    mix = mix.reshape(count, width).astype(jnp.bfloat16)
    mid = x_rows + jnp.dot(mix, w_out, preferred_element_type=jnp.float32)
    routed = norm_rows(mid, gain_two).astype(jnp.bfloat16)
    logits = jnp.dot(routed, w_router, preferred_element_type=jnp.float32)
    pick = flat_ids[:, :, None] == jnp.arange(experts_all, dtype=jnp.int32)[None, None, :]
    chosen = jnp.sum(jnp.where(pick, logits[:, None, :], 0.0), -1)
    expo_gate = jnp.exp(chosen)
    gates = expo_gate / jnp.sum(expo_gate, -1, keepdims=True)
    pair_ids = flat_ids.reshape(-1)
    hits = (pair_ids[:, None] == jnp.arange(experts_all, dtype=jnp.int32)[None, :]).astype(
        jnp.int32
    )
    before = jnp.cumsum(hits, 0) - hits
    slots = jnp.sum(before * hits, 1)
    where_rows = pair_ids * capacity + slots
    sent = jnp.repeat(routed, TOP, axis=0)
    buffer = jnp.zeros((experts_all * capacity, width), jnp.bfloat16).at[where_rows].set(sent)
    buffer = buffer.reshape(experts_all, capacity, width)
    arrived = lax.all_to_all(buffer, "expert", split_axis=0, concat_axis=1, tiled=True)
    pre = jnp.einsum("erd,edf->erf", arrived, w_in, preferred_element_type=jnp.float32)
    act = smooth_gelu(pre).astype(jnp.bfloat16)
    made = jnp.einsum("erf,efd->erd", act, w_back, preferred_element_type=jnp.float32).astype(
        jnp.bfloat16
    )
    returned = lax.all_to_all(made, "expert", split_axis=1, concat_axis=0, tiled=True)
    picked = returned.reshape(experts_all * capacity, width)[where_rows].reshape(count, TOP, width)
    output = mid + jnp.sum(gates[:, :, None] * picked.astype(jnp.float32), 1)
    return (
        x_rows,
        normed,
        query4,
        keys4,
        vals4,
        probs,
        probs_low,
        mix,
        mid,
        routed,
        pick,
        gates,
        where_rows,
        arrived,
        pre,
        act,
        picked,
        output,
        capacity,
    )


def shards(
    tokens, gain_one, w_qkv, w_out, gain_two, w_router, w_in, w_back, route_ids, key_mask, cotangent
):
    nimg, half, width = tokens.shape
    count = nimg * half
    experts_all = w_router.shape[1]
    flat_ids = route_ids.reshape(count, TOP)
    live = key_mask > 0
    state = forward(
        tokens, gain_one, w_qkv, w_out, gain_two, w_router, w_in, w_back, flat_ids, live
    )
    mixed = state[17].reshape(nimg, half, width).astype(jnp.bfloat16)
    state = forward(
        tokens, gain_one, w_qkv, w_out, gain_two, w_router, w_in, w_back, flat_ids, live
    )
    (
        x_rows,
        normed,
        query4,
        keys4,
        vals4,
        probs,
        probs_low,
        mix,
        mid,
        routed,
        pick,
        gates,
        where_rows,
        arrived,
        pre,
        act,
        picked,
        output,
        capacity,
    ) = state
    scale = HEAD_DIM ** (-0.5)
    high = lax.Precision.HIGHEST
    grad_y = cotangent.astype(jnp.float32).reshape(count, width)
    grad_gate = jnp.sum(grad_y[:, None, :] * picked.astype(jnp.float32), -1)
    d_out = (
        (gates[:, :, None] * grad_y[:, None, :]).astype(jnp.bfloat16).reshape(count * TOP, width)
    )
    grad_buffer = jnp.zeros((experts_all * capacity, width), jnp.bfloat16).at[where_rows].set(d_out)
    grad_buffer = grad_buffer.reshape(experts_all, capacity, width)
    grad_arrived = lax.all_to_all(grad_buffer, "expert", split_axis=0, concat_axis=1, tiled=True)
    d_act = jnp.einsum("erd,efd->erf", grad_arrived, w_back, preferred_element_type=jnp.float32)
    grad_back = jnp.einsum("erf,erd->efd", act, grad_arrived, preferred_element_type=jnp.float32)
    _, gelu_pull = jax.vjp(smooth_gelu, pre)
    d_pre = gelu_pull(d_act)[0].astype(jnp.bfloat16)
    grad_in = jnp.einsum("erd,erf->edf", arrived, d_pre, preferred_element_type=jnp.float32)
    d_in = jnp.einsum("erf,edf->erd", d_pre, w_in, preferred_element_type=jnp.float32).astype(
        jnp.bfloat16
    )
    grad_returned = lax.all_to_all(d_in, "expert", split_axis=1, concat_axis=0, tiled=True)
    grad_rows = grad_returned.reshape(experts_all * capacity, width)[where_rows].reshape(
        count, TOP, width
    )
    d_experts = jnp.sum(grad_rows.astype(jnp.float32), 1)
    d_chosen = gates * (grad_gate - jnp.sum(gates * grad_gate, -1, keepdims=True))
    d_logits = jnp.sum(jnp.where(pick, d_chosen[:, :, None], 0.0), 1)
    grad_router = jnp.dot(routed.astype(jnp.float32).T, d_logits, precision=high)
    d_routed = d_experts + jnp.dot(d_logits, w_router.astype(jnp.float32).T, precision=high)
    _, norm_two_pull = jax.vjp(norm_rows, mid, gain_two)
    d_mid_norm, grad_gain_two = norm_two_pull(d_routed)
    d_mid = grad_y + d_mid_norm
    d_branch = d_mid.astype(jnp.bfloat16)
    grad_out = jnp.einsum("td,te->de", mix, d_branch, preferred_element_type=jnp.float32)
    d_mix = jnp.dot(d_branch, w_out.T, preferred_element_type=jnp.float32).astype(jnp.bfloat16)
    d_mix4 = d_mix.reshape(nimg, half, HEADS, HEAD_DIM)
    d_probs = jnp.einsum("iqhc,ikhc->ihqk", d_mix4, vals4, preferred_element_type=jnp.float32)
    d_scores = (probs * (d_probs - jnp.sum(probs * d_probs, -1, keepdims=True))).astype(
        jnp.bfloat16
    )
    d_query = (
        jnp.einsum("ihqk,ikhc->iqhc", d_scores, keys4, preferred_element_type=jnp.float32) * scale
    )
    d_keys = (
        jnp.einsum("ihqk,iqhc->ikhc", d_scores, query4, preferred_element_type=jnp.float32) * scale
    )
    d_vals = jnp.einsum("ihqk,iqhc->ikhc", probs_low, d_mix4, preferred_element_type=jnp.float32)
    seq = keys4.shape[1]
    d_keys_own, d_vals_own = (
        lax.psum_scatter(
            d_keys.reshape(nimg, seq, width).astype(jnp.bfloat16),
            "ctx",
            scatter_dimension=1,
            tiled=True,
        ).astype(jnp.float32),
        lax.psum_scatter(
            d_vals.reshape(nimg, seq, width).astype(jnp.bfloat16),
            "ctx",
            scatter_dimension=1,
            tiled=True,
        ).astype(jnp.float32),
    )
    d_qkv = jnp.concatenate(
        [
            d_query.reshape(count, width).astype(jnp.bfloat16),
            d_keys_own.reshape(count, width).astype(jnp.bfloat16),
            d_vals_own.reshape(count, width).astype(jnp.bfloat16),
        ],
        axis=1,
    )
    grad_qkv = jnp.einsum("td,te->de", normed, d_qkv, preferred_element_type=jnp.float32)
    d_normed = jnp.dot(d_qkv, w_qkv.T, preferred_element_type=jnp.float32)
    _, norm_one_pull = jax.vjp(norm_rows, x_rows, gain_one)
    d_x_norm, grad_gain_one = norm_one_pull(d_normed)
    grad_tokens = (d_mid + d_x_norm).reshape(nimg, half, width).astype(jnp.bfloat16)
    grad_gain_one, grad_qkv, grad_out, grad_gain_two, grad_router = lax.psum(
        (grad_gain_one, grad_qkv, grad_out, grad_gain_two, grad_router), ("dp", "ctx", "expert")
    )
    grad_in, grad_back = (
        lax.psum(grad_in.astype(jnp.bfloat16), ("dp", "ctx")).astype(jnp.float32),
        lax.psum(grad_back.astype(jnp.bfloat16), ("dp", "ctx")).astype(jnp.float32),
    )
    return (
        mixed,
        grad_tokens,
        grad_gain_one,
        grad_qkv,
        grad_out,
        grad_gain_two,
        grad_router,
        grad_in,
        grad_back,
    )


def solution(mesh):
    placed = (
        P(("dp", "expert"), "ctx", None),
        P(),
        P(),
        P(),
        P(),
        P(),
        P("expert", None, None),
        P("expert", None, None),
        P(("dp", "expert"), "ctx", None, None, None),
        P(("dp", "expert"), None),
        P(("dp", "expert"), "ctx", None),
    )
    return jax.shard_map(
        shards,
        mesh=mesh,
        in_specs=placed,
        out_specs=(
            P(("dp", "expert"), "ctx", None),
            P(("dp", "expert"), "ctx", None),
            P(),
            P(),
            P(),
            P(),
            P(),
            P("expert", None, None),
            P("expert", None, None),
        ),
        check_vma=False,
    )
```

profile of v0, /device:TPU:0, one launch (start us, length us, event | category | flops | bytes accessed | tf_op | source)
XLA Modules:
  0.0 711.9 jit_solution(9703908839708034771)
XLA Ops:
  40.1 6.3 fusion.48
  64.7 14.4 %scatter_custom_fusion.1 = bf16[2400,512]{1,0:T(8,128)(2,1)} fusion(s32[1200]{0:T(1024)S(1)} %fusion.39, f32[1200,512]{1,0:T(8,128)} %mul.324, f32[1200]{0:T(1024)S(1)} %div.90, bf16[]{:T(256)} %constant.40.clone.1), kind=kCustom, calls=%fused_computation.58 | custom fusion | flops 1228800 | bytes 4923394 | tf_op jit(solution)/shard_map/scatter | solution.py:145
  79.0 4.9 all-to-all-start.2
  89.5 10.2 %scatter_custom_fusion = bf16[2400,512]{1,0:T(8,128)(2,1)} fusion(s32[1200]{0:T(1024)S(1)} %fusion.39, bf16[1200,512]{1,0:T(8,128)(2,1)} %reshape.409, bf16[]{:T(256)} %constant.40.clone.1), kind=kCustom, calls=%fused_computation.68 | custom fusion | bytes 2458112 | tf_op jit(solution)/shard_map/scatter | solution.py:68
  99.7 40.7 %all-to-all-done.2 = bf16[4,600,512]{2,1,0:T(8,128)(2,1)} async-done(((bf16[4,600,512]{2,1,0:T(8,128)(2,1)}), bf16[4,600,512]{2,1,0:T(8,128)(2,1)}, u32[]{:S(2)}, u32[]{:S(2)}) %all-to-all-start.2) | async-done | bytes 2457632 | tf_op jit(solution)/shard_map/all_to_all | solution.py:147
  140.4 4.8 all-to-all-start
  145.2 11.4 %fusion.15 = f32[2400,2048]{1,0:T(8,128)} fusion(bf16[2400,512]{1,0:T(8,128)(2,1)} %bitcast.11, bf16[1,2048,512]{2,1,0:T(8,128)(2,1)} %param.18), kind=kOutput, calls=%fused_computation.40 | convolution fusion | flops 5033164800 | bytes 24215552 | tf_op jit(solution)/shard_map/erd,efd->erf/dot_general | solution.py:148
  156.6 44.1 %all-to-all-done = bf16[4,600,512]{2,1,0:T(8,128)(2,1)} async-done(((bf16[4,600,512]{2,1,0:T(8,128)(2,1)}), bf16[4,600,512]{2,1,0:T(8,128)(2,1)}, u32[]{:S(2)}, u32[]{:S(2)}) %all-to-all-start) | async-done | bytes 2457632 | tf_op jit(solution)/shard_map/all_to_all | solution.py:70
  200.8 24.4 %fusion.4 = (bf16[2400,2048]{1,0:T(8,128)(2,1)}, bf16[2400,2048]{1,0:T(8,128)(2,1)S(1)}) fusion(f32[2400,2048]{1,0:T(8,128)} %fusion.15, bf16[2400,512]{1,0:T(8,128)(2,1)} %bitcast.6, bf16[1,512,2048]{2,1,0:T(8,128)(2,1)S(1)} %copy-done), kind=kOutput, calls=%fused_computation.12 | convolution fusion | flops 5160960000 | bytes 43876352 | tf_op jit(solution)/shard_map/erd,edf->erf/dot_general | solution.py:71
  225.2 5.5 fusion.7
  230.7 21.7 %copy.149 = bf16[1,2400,512]{2,0,1:T(2,128)(2,1)} copy(bf16[1,2400,512]{2,1,0:T(8,128)(2,1)S(1)} %fusion.7) | data formatting | bytes 4915200 | tf_op jit(solution)/shard_map/convert_element_type | solution.py:73
  252.9 17.7 %reduce.11 = bf16[2400,512]{1,0:T(8,128)(2,1)} reduce(bf16[2400,1,512]{2,1,0:T(2,128)(2,1)} %bitcast.107, bf16[]{:T(256)} %broadcast.269), dimensions={1}, to_apply=%bitcast.101.reduce_sub_computation | reduce | bytes 4915202
  274.9 4.9 all-to-all-start.1
  279.9 9.4 %fusion.8 = bf16[1,2400,512]{2,1,0:T(8,128)(2,1)S(1)} fusion(bf16[2400,2048]{1,0:T(8,128)(2,1)} %get-tuple-element.28, bf16[1,512,2048]{2,1,0:T(8,128)(2,1)S(1)} %copy-done), kind=kOutput, calls=%fused_computation.23 | convolution fusion | flops 5034393600 | bytes 14385152 | tf_op jit(solution)/shard_map/erf,edf->erd/dot_general | solution.py:153
  289.2 21.7 %copy.148 = bf16[1,2400,512]{2,0,1:T(2,128)(2,1)} copy(bf16[1,2400,512]{2,1,0:T(8,128)(2,1)S(1)} %fusion.8) | data formatting | bytes 4915200 | tf_op jit(solution)/shard_map/convert_element_type | solution.py:153
  310.9 16.3 %reduce.10 = bf16[2400,512]{1,0:T(8,128)(2,1)S(1)} reduce(bf16[2400,1,512]{2,1,0:T(2,128)(2,1)} %bitcast.108, bf16[]{:T(256)} %broadcast.269), dimensions={1}, to_apply=%bitcast.100.reduce_sub_computation | reduce | bytes 4915202
  329.6 5.7 all-to-all-done.1
  335.3 4.5 all-to-all-start.3
  340.0 5.5 reshape.435
  348.6 4.7 gather_fusion
  357.3 7.2 %multiply_reduce_fusion.1 = (f32[600,2]{1,0:T(8,128)S(1)}, f32[600,512]{1,0:T(8,128)}) fusion(f32[600,2,512]{2,1,0:T(2,128)} %reshape.385, f32[600,512]{1,0:T(8,128)S(1)} %copy-done.5, f32[600,2]{1,0:T(8,128)S(1)} %copy.113), kind=kLoop, calls=%fused_computation.33 | loop fusion | flops 2149200 | bytes 4924800 | tf_op jit(solution)/shard_map/reduce_sum | solution.py:141
  364.7 30.7 %all-to-all-done.3 = bf16[4,2,153600]{2,1,0:T(2,128)(2,1)} async-done(((bf16[4,2,153600]{2,1,0:T(2,128)(2,1)}), bf16[4,2,153600]{2,1,0:T(2,128)(2,1)}, u32[]{:S(2)}, u32[]{:S(2)}) %all-to-all-start.3) | async-done | bytes 2457632 | tf_op jit(solution)/shard_map/all_to_all | solution.py:156
  395.4 5.3 reshape.437
  403.8 4.7 gather_fusion.1
  412.6 4.7 reduce_sum.196
  423.3 4.5 multiply_reduce_fusion
  442.2 10.2 %fusion.10 = bf16[1,512,2048]{2,1,0:T(8,128)(2,1)} fusion(bf16[2400,512]{1,0:T(8,128)(2,1)} %bitcast.6, bf16[2400,2048]{1,0:T(8,128)(2,1)} %get-tuple-element.28), kind=kOutput, calls=%fused_computation.29 | convolution fusion | flops 5034213376 | bytes 14385152 | tf_op jit(solution)/shard_map/erd,erf->edf/dot_general | solution.py:152
  452.5 10.0 %fusion.11 = bf16[1,2048,512]{2,1,0:T(8,128)(2,1)} fusion(bf16[2400,2048]{1,0:T(8,128)(2,1)} %copy-done.36, bf16[2400,512]{1,0:T(8,128)(2,1)} %bitcast.11), kind=kOutput, calls=%fused_computation.30 | convolution fusion | flops 5034213376 | bytes 14385152 | tf_op jit(solution)/shard_map/erf,erd->efd/dot_general | solution.py:149
  477.7 4.9 fusion.30
  482.6 67.8 %all-reduce.13.cloned.1.call-done = (bf16[1,512,2048]{2,1,0:T(8,128)(2,1)}, bf16[1,2048,512]{2,1,0:T(8,128)(2,1)}) async-done(((bf16[1,512,2048]{2,1,0:T(8,128)(2,1)}, bf16[1,2048,512]{2,1,0:T(8,128)(2,1)}), (bf16[1,512,2048]{2,1,0:T(8,128)(2,1)}, bf16[1,2048,512]{2,1,0:T(8,128)(2,1)})) %all-reduce.13.cloned.1.call-update) | async-done | bytes 4194320 | tf_op jit(solution)/shard_map/psum | solution.py:215
  564.9 39.8 %all-reduce.3 = (f32[512]{0:T(512)}, f32[512]{0:T(512)}, f32[512,4]{0,1:T(4,128)}) all-reduce(f32[512]{0:T(512)S(1)} %get-tuple-element.11, f32[512]{0:T(512)S(1)} %get-tuple-element.9, f32[512,4]{0,1:T(4,128)S(1)} %fusion.51), channel_id=1, replica_groups=mesh['dp'=4,'ctx'=2,'expert'=4] {'dp','ctx','expert'}, use_global_device_ids=true, to_apply=%region_26.27 | all-reduce | flops 3072 | bytes 24576 | tf_op jit(solution)/shard_map/psum | solution.py:211
  604.7 95.5 %all-reduce.11.cloned.1.call-done = (f32[512,1536]{1,0:T(8,128)}, f32[512,512]{1,0:T(8,128)}) async-done(((f32[512,1536]{1,0:T(8,128)}, f32[512,512]{1,0:T(8,128)}), (f32[512,1536]{1,0:T(8,128)}, f32[512,512]{1,0:T(8,128)})) %all-reduce.11.cloned.1.call-update) | async-done | bytes 4194320 | tf_op jit(solution)/shard_map/psum | solution.py:211
  (192 shorter events, 132.4 us)
Async XLA Ops:
  7.2 193.6 %copy-start = (bf16[1,512,2048]{2,1,0:T(8,128)(2,1)S(1)}, bf16[1,512,2048]{2,1,0:T(8,128)(2,1)}, u32[]{:S(2)}) copy-start(bf16[1,512,2048]{2,1,0:T(8,128)(2,1)} %param.17) | copy-start | bytes 6291460
  7.2 5.3 copy-start.32
  7.2 28.9 %all-gather.5.cloned.1.call-start = ((), (), s32[]{:S(2)}) async-start(), calls=%async_computation.5 | async-start | bytes 2457600 | tf_op jit(solution)/shard_map/all_gather | solution.py:34
  9.8 6.5 copy-start.9
  11.8 4.5 copy-start.26
  11.9 4.5 copy-start.23
  22.8 26.0 %all-gather.3.cloned.1.call-start = ((), (), s32[]{:S(2)}) async-start(), calls=%async_computation.4 | async-start | bytes 2457600 | tf_op jit(solution)/shard_map/all_gather | solution.py:35
  29.4 6.6 copy-start.4
  31.7 4.4 copy-start.31
  36.0 4.1 copy-start.16
  56.7 4.1 copy-start.10
  63.9 20.0 %copy-start.12 = (bf16[600,512]{1,0:T(8,128)(2,1)}, bf16[600,512]{1,0:T(8,128)(2,1)S(1)}, u32[]{:S(2)}) copy-start(bf16[600,512]{1,0:T(8,128)(2,1)S(1)} %multiply_convert_fusion.6) | copy-start | bytes 1843204
  79.0 61.3 %all-to-all-start.2 = ((bf16[4,600,512]{2,1,0:T(8,128)(2,1)}), bf16[4,600,512]{2,1,0:T(8,128)(2,1)}, u32[]{:S(2)}, u32[]{:S(2)}) async-start(bf16[4,600,512]{2,1,0:T(8,128)(2,1)} %bitcast.109), calls=%async_computation.2 | async-start | bytes 4915200 | tf_op jit(solution)/shard_map/all_to_all | solution.py:147
  140.4 60.4 %all-to-all-start = ((bf16[4,600,512]{2,1,0:T(8,128)(2,1)}), bf16[4,600,512]{2,1,0:T(8,128)(2,1)}, u32[]{:S(2)}, u32[]{:S(2)}) async-start(bf16[4,600,512]{2,1,0:T(8,128)(2,1)} %bitcast.110), calls=%async_computation | async-start | bytes 4915200 | tf_op jit(solution)/shard_map/all_to_all | solution.py:70
  200.8 24.4 %copy-start.34 = (bf16[1,2048,512]{2,1,0:T(8,128)(2,1)S(1)}, bf16[1,2048,512]{2,1,0:T(8,128)(2,1)}, u32[]{:S(2)}) copy-start(bf16[1,2048,512]{2,1,0:T(8,128)(2,1)} %param.18) | copy-start | bytes 6291460
  225.2 5.5 copy-start.36
  274.9 60.4 %all-to-all-start.1 = ((bf16[4,2,153600]{2,1,0:T(2,128)(2,1)}), bf16[4,2,153600]{2,1,0:T(2,128)(2,1)}, u32[]{:S(2)}, u32[]{:S(2)}) async-start(bf16[4,2,153600]{2,1,0:T(2,128)(2,1)} %reshape.434), calls=%async_computation.1 | async-start | bytes 4915200 | tf_op jit(solution)/shard_map/all_to_all | solution.py:76
  335.3 60.0 %all-to-all-start.3 = ((bf16[4,2,153600]{2,1,0:T(2,128)(2,1)}), bf16[4,2,153600]{2,1,0:T(2,128)(2,1)}, u32[]{:S(2)}, u32[]{:S(2)}) async-start(bf16[4,2,153600]{2,1,0:T(2,128)(2,1)} %reshape.436), calls=%async_computation.3 | async-start | bytes 4915200 | tf_op jit(solution)/shard_map/all_to_all | solution.py:156
  339.9 130.6 %all-reduce.15.cloned.1.call-start = ((), (), s32[]{:S(2)}) async-start(), calls=%async_computation.8 | async-start | bytes 4915200
  412.6 4.7 copy-start.3
  421.2 6.6 slice-start
  423.3 4.6 slice-start.1
  442.2 108.3 %all-reduce.13.cloned.1.call-start = ((), (), s32[]{:S(2)}) async-start(), calls=%async_computation.7 | async-start | bytes 8388608 | tf_op jit(solution)/shard_map/psum | solution.py:215
  462.4 237.8 %all-reduce.11.cloned.1.call-start = ((), (), s32[]{:S(2)}) async-start(), calls=%async_computation.6 | async-start | bytes 8388608 | tf_op jit(solution)/shard_map/psum | solution.py:211
  473.1 4.6 copy-start.11
  473.1 4.6 copy-start.27
  473.1 4.6 copy-start.29
  473.1 4.6 copy-start.33
  477.7 4.9 copy-start.21
  550.5 4.3 copy-start.18
  554.7 4.6 copy-start.13
  700.2 4.9 copy-start.1
  (16 other events, 33.8 us)
Sparse Core Ops, SparseCore 0:
  22.9 12.5 all-gather.4
  37.6 11.0 all-gather.2
  442.3 21.3 all-reduce.14
  468.0 82.3 all-reduce.12
  557.5 142.6 all-reduce.10
where the time goes:
time: 716 us; the launch traced here: 712 us
  waiting for transfers between devices  287 us (40%)
  local copies, waits for them, and re-layouts  160 us (22%)
  matrix products  112 us (16%)
  other arithmetic  78.6 us (11%)
  blocking collectives  39.8 us (6%)
  starting transfers between devices  19.8 us (3%)
  between operations  15.4 us (2%)
    psum x1, waiting for transfers between devices, shards(): lax.psum((grad_gain_one, grad_qkv, grad_out, grad_gain_two, grad_router),...  95.5 us
    psum x1, waiting for transfers between devices, shards(): lax.psum(grad_in.astype(jnp.bfloat16), ('dp', 'ctx')).astype(jnp.float32)  67.8 us
    all_to_all x1, waiting for transfers between devices, forward(): lax.all_to_all(buffer, 'expert', split_axis=0, concat_axis=1, tiled=True)  44.1 us
    all_to_all x1, waiting for transfers between devices, shards(): lax.all_to_all(grad_buffer, 'expert', split_axis=0, concat_axis=1, tiled=...  40.7 us
    psum x1, blocking collectives, shards(): lax.psum((grad_gain_one, grad_qkv, grad_out, grad_gain_two, grad_router),...  39.8 us
    unnamed x94, local copies, waits for them, and re-layouts  36.9 us
    unnamed x4, other arithmetic  34.1 us
    all_to_all x1, waiting for transfers between devices, shards(): lax.all_to_all(d_in, 'expert', split_axis=1, concat_axis=0, tiled=True)  30.7 us
  transfers between devices with their start and end apart: 9, of which 7 were waited for; matrix products, arithmetic and copies ran while one was open for 25% of the time, Pallas kernels for 0%

commit v1 on v0

--- a/solution.py
+++ b/solution.py
@@ -212,7 +212,7 @@
         (grad_gain_one, grad_qkv, grad_out, grad_gain_two, grad_router), ("dp", "ctx", "expert")
     )
     grad_in, grad_back = (
-        lax.psum(grad_in.astype(jnp.bfloat16), ("dp", "ctx")).astype(jnp.float32),
+        lax.psum(lax.psum(grad_in.astype(jnp.bfloat16), "ctx"), "dp").astype(jnp.float32),
         lax.psum(grad_back.astype(jnp.bfloat16), ("dp", "ctx")).astype(jnp.float32),
     )
     return (

time: 716 us -> 776 us (1.084)
  waiting for transfers between devices: 287 us -> 345 us
    psum x1, waiting for transfers between devices: 95.5 us -> 144 us  [shards(): lax.psum((grad_gain_one, grad_qkv, grad_out, grad_gain_two, grad_router),...]
    unnamed x6 -> x7, waiting for transfers between devices: 0.08 us -> 18.5 us
    all_to_all x1, waiting for transfers between devices: 30.7 us -> 20.5 us  [shards(): lax.all_to_all(d_in, 'expert', split_axis=1, concat_axis=0, tiled=True)]
    unnamed x94 -> x96, local copies, waits for them, and re-layouts: 36.9 us -> 35.3 us
    psum x1 -> x2, waiting for transfers between devices: 67.8 us -> 69.1 us  [the longest x1 47.7 us: shards(): lax.psum(grad_back.astype(jnp.bfloat16), ('dp', 'ctx')).astype(jnp.float32)]
  transfers between devices with their start and end apart: 9 -> 10, of which waited for: 7 -> 9; matrix products, arithmetic and copies ran while one was open for 25% -> 23% of each run, Pallas kernels for 0% -> 0%
where the time goes in v1:
time: 776 us; the launch traced here: 771 us
  waiting for transfers between devices  345 us (44%)
  local copies, waits for them, and re-layouts  158 us (20%)
  matrix products  113 us (15%)
  other arithmetic  80.4 us (10%)
  blocking collectives  39.4 us (5%)
  starting transfers between devices  19.4 us (2%)
  between operations  15.7 us (2%)
    psum x1, waiting for transfers between devices, shards(): lax.psum((grad_gain_one, grad_qkv, grad_out, grad_gain_two, grad_router),...  144 us
    psum x1, waiting for transfers between devices, shards(): lax.psum(grad_back.astype(jnp.bfloat16), ('dp', 'ctx')).astype(jnp.float32)  47.7 us
    all_to_all x1, waiting for transfers between devices, forward(): lax.all_to_all(buffer, 'expert', split_axis=0, concat_axis=1, tiled=True)  44.2 us
    all_to_all x1, waiting for transfers between devices, shards(): lax.all_to_all(grad_buffer, 'expert', split_axis=0, concat_axis=1, tiled=...  40.7 us
    psum x1, blocking collectives, shards(): lax.psum((grad_gain_one, grad_qkv, grad_out, grad_gain_two, grad_router),...  39.4 us
    unnamed x96, local copies, waits for them, and re-layouts  35.3 us
    unnamed x4, other arithmetic  34.1 us
    dot_general x1, matrix products, forward(): jnp.einsum('erd,edf->erf', arrived, w_in, preferred_element_type=jnp.floa...  24.4 us
  transfers between devices with their start and end apart: 10, of which 9 were waited for; matrix products, arithmetic and copies ran while one was open for 23% of the time, Pallas kernels for 0%

profile of v1, /device:TPU:0, one launch (start us, length us, event | category | flops | bytes accessed | tf_op | source)
XLA Modules:
  0.0 771.2 jit_solution(15100873590402025199)
XLA Ops:
  40.0 6.3 fusion.48
  64.7 14.7 %scatter_custom_fusion.1 = bf16[2400,512]{1,0:T(8,128)(2,1)} fusion(s32[1200]{0:T(1024)S(1)} %fusion.39, f32[1200,512]{1,0:T(8,128)} %mul.324, f32[1200]{0:T(1024)S(1)} %div.90, bf16[]{:T(256)} %constant.40.clone.1), kind=kCustom, calls=%fused_computation.58 | custom fusion | flops 1228800 | bytes 4923394 | tf_op jit(solution)/shard_map/scatter | solution.py:145
  79.4 4.9 all-to-all-start.2
  89.8 10.2 %scatter_custom_fusion = bf16[2400,512]{1,0:T(8,128)(2,1)} fusion(s32[1200]{0:T(1024)S(1)} %fusion.39, bf16[1200,512]{1,0:T(8,128)(2,1)} %reshape.409, bf16[]{:T(256)} %constant.40.clone.1), kind=kCustom, calls=%fused_computation.68 | custom fusion | bytes 2458112 | tf_op jit(solution)/shard_map/scatter | solution.py:68
  100.0 40.7 %all-to-all-done.2 = bf16[4,600,512]{2,1,0:T(8,128)(2,1)} async-done(((bf16[4,600,512]{2,1,0:T(8,128)(2,1)}), bf16[4,600,512]{2,1,0:T(8,128)(2,1)}, u32[]{:S(2)}, u32[]{:S(2)}) %all-to-all-start.2) | async-done | bytes 2457632 | tf_op jit(solution)/shard_map/all_to_all | solution.py:147
  140.7 4.7 all-to-all-start
  145.5 11.4 %fusion.15 = f32[2400,2048]{1,0:T(8,128)} fusion(bf16[2400,512]{1,0:T(8,128)(2,1)} %bitcast.11, bf16[1,2048,512]{2,1,0:T(8,128)(2,1)} %param.18), kind=kOutput, calls=%fused_computation.40 | convolution fusion | flops 5033164800 | bytes 24215552 | tf_op jit(solution)/shard_map/erd,efd->erf/dot_general | solution.py:148
  156.9 44.2 %all-to-all-done = bf16[4,600,512]{2,1,0:T(8,128)(2,1)} async-done(((bf16[4,600,512]{2,1,0:T(8,128)(2,1)}), bf16[4,600,512]{2,1,0:T(8,128)(2,1)}, u32[]{:S(2)}, u32[]{:S(2)}) %all-to-all-start) | async-done | bytes 2457632 | tf_op jit(solution)/shard_map/all_to_all | solution.py:70
  201.1 24.4 %fusion.4 = (bf16[2400,2048]{1,0:T(8,128)(2,1)}, bf16[2400,2048]{1,0:T(8,128)(2,1)S(1)}) fusion(f32[2400,2048]{1,0:T(8,128)} %fusion.15, bf16[2400,512]{1,0:T(8,128)(2,1)} %bitcast.6, bf16[1,512,2048]{2,1,0:T(8,128)(2,1)S(1)} %copy-done), kind=kOutput, calls=%fused_computation.12 | convolution fusion | flops 5160960000 | bytes 43876352 | tf_op jit(solution)/shard_map/erd,edf->erf/dot_general | solution.py:71
  225.5 5.5 fusion.7
  231.0 21.7 %copy.149 = bf16[1,2400,512]{2,0,1:T(2,128)(2,1)} copy(bf16[1,2400,512]{2,1,0:T(8,128)(2,1)S(1)} %fusion.7) | data formatting | bytes 4915200 | tf_op jit(solution)/shard_map/convert_element_type | solution.py:73
  253.2 17.7 %reduce.11 = bf16[2400,512]{1,0:T(8,128)(2,1)} reduce(bf16[2400,1,512]{2,1,0:T(2,128)(2,1)} %bitcast.107, bf16[]{:T(256)} %broadcast.269), dimensions={1}, to_apply=%bitcast.101.reduce_sub_computation | reduce | bytes 4915202
  275.2 4.8 all-to-all-start.1
  280.0 9.4 %fusion.8 = bf16[1,2400,512]{2,1,0:T(8,128)(2,1)S(1)} fusion(bf16[2400,2048]{1,0:T(8,128)(2,1)} %get-tuple-element.27, bf16[1,512,2048]{2,1,0:T(8,128)(2,1)S(1)} %copy-done), kind=kOutput, calls=%fused_computation.23 | convolution fusion | flops 5034393600 | bytes 14385152 | tf_op jit(solution)/shard_map/erf,edf->erd/dot_general | solution.py:153
  289.4 21.7 %copy.148 = bf16[1,2400,512]{2,0,1:T(2,128)(2,1)} copy(bf16[1,2400,512]{2,1,0:T(8,128)(2,1)S(1)} %fusion.8) | data formatting | bytes 4915200 | tf_op jit(solution)/shard_map/convert_element_type | solution.py:153
  311.0 16.3 %reduce.10 = bf16[2400,512]{1,0:T(8,128)(2,1)S(1)} reduce(bf16[2400,1,512]{2,1,0:T(2,128)(2,1)} %bitcast.108, bf16[]{:T(256)} %broadcast.269), dimensions={1}, to_apply=%bitcast.100.reduce_sub_computation | reduce | bytes 4915202
  329.8 5.7 all-to-all-done.1
  340.1 10.4 %fusion.10 = bf16[1,512,2048]{2,1,0:T(8,128)(2,1)} fusion(bf16[2400,512]{1,0:T(8,128)(2,1)} %bitcast.6, bf16[2400,2048]{1,0:T(8,128)(2,1)} %get-tuple-element.27), kind=kOutput, calls=%fused_computation.29 | convolution fusion | flops 5034213376 | bytes 14385152 | tf_op jit(solution)/shard_map/erd,erf->edf/dot_general | solution.py:152
  350.5 5.3 reshape.435
  358.9 4.7 gather_fusion
  367.6 7.2 multiply_reduce_fusion.1
  375.0 20.5 %all-to-all-done.3 = bf16[4,2,153600]{2,1,0:T(2,128)(2,1)} async-done(((bf16[4,2,153600]{2,1,0:T(2,128)(2,1)}), bf16[4,2,153600]{2,1,0:T(2,128)(2,1)}, u32[]{:S(2)}, u32[]{:S(2)}) %all-to-all-start.3) | async-done | bytes 2457632 | tf_op jit(solution)/shard_map/all_to_all | solution.py:156
  395.5 5.3 reshape.437
  404.0 4.7 gather_fusion.1
  412.7 4.7 reduce_sum.196
  442.4 10.2 %fusion.11 = bf16[1,2048,512]{2,1,0:T(8,128)(2,1)} fusion(bf16[2400,2048]{1,0:T(8,128)(2,1)} %copy-done.37, bf16[2400,512]{1,0:T(8,128)(2,1)} %bitcast.11), kind=kOutput, calls=%fused_computation.30 | convolution fusion | flops 5034213376 | bytes 14385152 | tf_op jit(solution)/shard_map/erf,erd->efd/dot_general | solution.py:149
  452.7 18.4 %all-reduce.17.cloned.1.call-done = (bf16[6,200,512]{2,1,0:T(8,128)(2,1)}, bf16[6,200,512]{2,1,0:T(8,128)(2,1)}, bf16[1,512,2048]{2,1,0:T(8,128)(2,1)}) async-done(((bf16[6,200,512]{2,1,0:T(8,128)(2,1)}, bf16[6,200,512]{2,1,0:T(8,128)(2,1)}, bf16[1,512,2048]{2,1,0:T(8,128)(2,1)}), (bf16[6,200,512]{2,1,0:T(8,128)(2,1)}, bf16[6,200,512]{2,1,0:T(8,128)(2,1)}, ...) | async-done | bytes 4554768
  485.1 4.9 fusion.30
  490.0 47.7 %all-reduce.13.cloned.1.call-done = bf16[1,2048,512]{2,1,0:T(8,128)(2,1)} async-done(((bf16[1,2048,512]{2,1,0:T(8,128)(2,1)}), bf16[1,2048,512]{2,1,0:T(8,128)(2,1)}) %all-reduce.13.cloned.1.call-update) | async-done | bytes 2097168 | tf_op jit(solution)/shard_map/psum | solution.py:216
  550.2 39.4 %all-reduce.3 = (f32[512]{0:T(512)}, f32[512]{0:T(512)}, f32[512,4]{0,1:T(4,128)}) all-reduce(f32[512]{0:T(512)S(1)} %get-tuple-element.11, f32[512]{0:T(512)S(1)} %get-tuple-element.9, f32[512,4]{0,1:T(4,128)S(1)} %fusion.51), channel_id=1, replica_groups=mesh['dp'=4,'ctx'=2,'expert'=4] {'dp','ctx','expert'}, use_global_device_ids=true, to_apply=%region_26.27 | all-reduce | flops 3072 | bytes 24576 | tf_op jit(solution)/shard_map/psum | solution.py:211
  589.6 21.3 %all-reduce.11.cloned.1.call-done = bf16[1,512,2048]{2,1,0:T(8,128)(2,1)} async-done(((bf16[1,512,2048]{2,1,0:T(8,128)(2,1)}), bf16[1,512,2048]{2,1,0:T(8,128)(2,1)}) %all-reduce.11.cloned.1.call-update) | async-done | bytes 2097168 | tf_op jit(solution)/shard_map/psum | solution.py:215
  615.1 144.1 %all-reduce.15.cloned.1.call-done = (f32[512,1536]{1,0:T(8,128)}, f32[512,512]{1,0:T(8,128)}) async-done(((f32[512,1536]{1,0:T(8,128)}, f32[512,512]{1,0:T(8,128)}), (f32[512,1536]{1,0:T(8,128)}, f32[512,512]{1,0:T(8,128)})) %all-reduce.15.cloned.1.call-update) | async-done | bytes 4194320 | tf_op jit(solution)/shard_map/psum | solution.py:211
  (197 shorter events, 142.3 us)
Async XLA Ops:
  7.2 193.9 %copy-start = (bf16[1,512,2048]{2,1,0:T(8,128)(2,1)S(1)}, bf16[1,512,2048]{2,1,0:T(8,128)(2,1)}, u32[]{:S(2)}) copy-start(bf16[1,512,2048]{2,1,0:T(8,128)(2,1)} %param.17) | copy-start | bytes 6291460
  7.2 5.3 copy-start.33
  7.2 28.8 %all-gather.5.cloned.1.call-start = ((), (), s32[]{:S(2)}) async-start(), calls=%async_computation.5 | async-start | bytes 2457600 | tf_op jit(solution)/shard_map/all_gather | solution.py:34
  9.8 6.5 copy-start.9
  11.8 4.5 copy-start.27
  11.9 4.5 copy-start.24
  22.8 26.0 %all-gather.3.cloned.1.call-start = ((), (), s32[]{:S(2)}) async-start(), calls=%async_computation.4 | async-start | bytes 2457600 | tf_op jit(solution)/shard_map/all_gather | solution.py:35
  29.2 6.6 copy-start.4
  31.5 4.4 copy-start.32
  63.9 20.3 %copy-start.12 = (bf16[600,512]{1,0:T(8,128)(2,1)}, bf16[600,512]{1,0:T(8,128)(2,1)S(1)}, u32[]{:S(2)}) copy-start(bf16[600,512]{1,0:T(8,128)(2,1)S(1)} %multiply_convert_fusion.6) | copy-start | bytes 1843204
  79.4 61.4 %all-to-all-start.2 = ((bf16[4,600,512]{2,1,0:T(8,128)(2,1)}), bf16[4,600,512]{2,1,0:T(8,128)(2,1)}, u32[]{:S(2)}, u32[]{:S(2)}) async-start(bf16[4,600,512]{2,1,0:T(8,128)(2,1)} %bitcast.109), calls=%async_computation.2 | async-start | bytes 4915200 | tf_op jit(solution)/shard_map/all_to_all | solution.py:147
  140.7 60.3 %all-to-all-start = ((bf16[4,600,512]{2,1,0:T(8,128)(2,1)}), bf16[4,600,512]{2,1,0:T(8,128)(2,1)}, u32[]{:S(2)}, u32[]{:S(2)}) async-start(bf16[4,600,512]{2,1,0:T(8,128)(2,1)} %bitcast.110), calls=%async_computation | async-start | bytes 4915200 | tf_op jit(solution)/shard_map/all_to_all | solution.py:70
  201.1 24.4 %copy-start.35 = (bf16[1,2048,512]{2,1,0:T(8,128)(2,1)S(1)}, bf16[1,2048,512]{2,1,0:T(8,128)(2,1)}, u32[]{:S(2)}) copy-start(bf16[1,2048,512]{2,1,0:T(8,128)(2,1)} %param.18) | copy-start | bytes 6291460
  225.5 5.5 copy-start.37
  275.2 60.2 %all-to-all-start.1 = ((bf16[4,2,153600]{2,1,0:T(2,128)(2,1)}), bf16[4,2,153600]{2,1,0:T(2,128)(2,1)}, u32[]{:S(2)}, u32[]{:S(2)}) async-start(bf16[4,2,153600]{2,1,0:T(2,128)(2,1)} %reshape.434), calls=%async_computation.1 | async-start | bytes 4915200 | tf_op jit(solution)/shard_map/all_to_all | solution.py:76
  335.5 60.0 %all-to-all-start.3 = ((bf16[4,2,153600]{2,1,0:T(2,128)(2,1)}), bf16[4,2,153600]{2,1,0:T(2,128)(2,1)}, u32[]{:S(2)}, u32[]{:S(2)}) async-start(bf16[4,2,153600]{2,1,0:T(2,128)(2,1)} %reshape.436), calls=%async_computation.3 | async-start | bytes 4915200 | tf_op jit(solution)/shard_map/all_to_all | solution.py:156
  340.0 131.1 %all-reduce.17.cloned.1.call-start = ((), (), s32[]{:S(2)}) async-start(), calls=%async_computation.9 | async-start | bytes 9109504
  412.7 4.7 copy-start.3
  421.4 6.6 slice-start
  423.4 4.6 slice-start.1
  442.4 95.4 %all-reduce.13.cloned.1.call-start = ((), (), s32[]{:S(2)}) async-start(), calls=%async_computation.7 | async-start | bytes 4194304 | tf_op jit(solution)/shard_map/psum | solution.py:216
  452.6 18.6 %copy-start.36 = (u32[32]{0:T(128)S(1)}, u32[32]{0:T(128)}, u32[]{:S(2)}) copy-start(u32[32]{0:T(128)} %constant.59) | copy-start | bytes 388
  452.7 158.3 %all-reduce.11.cloned.1.call-start = ((), (), s32[]{:S(2)}) async-start(), calls=%async_computation.6 | async-start | bytes 4194304 | tf_op jit(solution)/shard_map/psum | solution.py:215
  471.2 288.0 %all-reduce.15.cloned.1.call-start = ((), (), s32[]{:S(2)}) async-start(), calls=%async_computation.8 | async-start | bytes 8388608 | tf_op jit(solution)/shard_map/psum | solution.py:211
  480.4 4.6 copy-start.11
  480.4 4.6 copy-start.28
  480.4 4.6 copy-start.30
  480.4 4.6 copy-start.34
  485.1 4.9 copy-start.20
  490.0 54.0 %copy-start.13 = (bf16[600,512]{1,0:T(8,128)(2,1)S(1)}, bf16[600,512]{1,0:T(8,128)(2,1)}, u32[]{:S(2)}) copy-start(bf16[600,512]{1,0:T(8,128)(2,1)} %copy-done.12) | copy-start | bytes 1843204
  544.3 4.2 copy-start.25
  759.2 4.9 copy-start.1
  (18 other events, 41.1 us)
Sparse Core Ops, SparseCore 0:
  22.9 12.5 all-gather.4
  37.6 11.0 all-gather.2
  442.5 28.6 all-reduce.16
  475.1 62.5 all-reduce.12
  541.0 69.9 all-reduce.10
  617.1 142.0 all-reduce.14
